TPU v7x, 32 devices: a whole 2x2x4 slice. The times are simulated.
32 devices in a mesh: ctx: 16 (over z, x, core), head: 2 (over y).
Axes of the slice: x: 2, y: 2, z: 4, core: 2. Of those that a mesh axis runs over, the one named last changes fastest.
Arguments:
- latent: bfloat16 [6144, 5120], P('ctx', 'head'), may hold values from -6 to 6
- probe: bfloat16 [6144, 5120], P('ctx'), may hold values from -6 to 6
- norm_gain: float32 [5120], replicated, may hold values from 0.25 to 1.75
- w_query: bfloat16 [5120, 3072], P('ctx', 'head'), may hold values from -2 to 2, as said below
- w_key: bfloat16 [5120, 3072], P('ctx', 'head'), may hold values from -2 to 2, as said below
- w_value: bfloat16 [5120, 3072], P('ctx', 'head'), may hold values from -0.078125 to 0.078125
- w_out: bfloat16 [3072, 5120], P('head', 'ctx'), may hold values from -0.109375 to 0.109375
- tile_mask: int32 [48, 48], replicated, may hold values from 0 to 1, as said below
Outputs:
- mixed: bfloat16 [6144, 5120], P('ctx', 'head')
- branch_tangent: bfloat16 [6144, 5120], P('ctx', 'head')
- trace_terms: float32 [6144], P('ctx')
Inputs may be any that keep to these rules, and one draw needn't show every extreme that they name: `tile_mask`: entry [q, k] is 0 where |q - k| > 3, and 1 where q == k or |q - k| == 3. `w_query`: entries of order 5120^-0.5. `w_key`: entries of order 5120^-0.5.
All inputs are finite; a program needn't handle non-finite values.
Results may differ from a plain program's by a relative error of at most 0.011.
Values may be sent and summed in bfloat16 or wider, within the bound.
A program may use at most 192 MiB of HBM per device.

v0:
```python
import jax
import jax.numpy as jnp
from jax import lax
from jax.sharding import PartitionSpec as P

D = 5120
HD = 128
TILE = 128


def with_halo(block, sides, width):
    for axis, dim in sides:
        count = lax.axis_size(axis)
        forward = [(i, i + 1) for i in range(count - 1)]
        backward = [(target, source) for source, target in forward]
        low = lax.ppermute(
            lax.slice_in_dim(block, block.shape[dim] - width, None, axis=dim), axis, forward
        )
        high = lax.ppermute(lax.slice_in_dim(block, 0, width, axis=dim), axis, backward)
        block = jnp.concatenate([low, block, high], axis=dim)
    return block


def attend_block(queries, queries_t, keys, values, keys_t, values_t, allowed):
    score_scale = HD ** (-0.5)
    scores = (
        jnp.einsum("qhd,khd->hqk", queries, keys, preferred_element_type=jnp.float32) * score_scale
    )
    masked = jnp.where(allowed[None], scores, -jnp.inf)
    highest = jnp.max(masked, -1, keepdims=True)
    expos = jnp.exp(masked - highest)
    probs = expos / jnp.sum(expos, -1, keepdims=True)
    scores_t = jnp.einsum("qhd,khd->hqk", queries_t, keys, preferred_element_type=jnp.float32)
    scores_t = (
        scores_t + jnp.einsum("qhd,khd->hqk", queries, keys_t, preferred_element_type=jnp.float32)
    ) * score_scale
    probs_t = probs * (scores_t - jnp.sum(probs * scores_t, -1, keepdims=True))
    probs_b = probs.astype(jnp.bfloat16)
    probs_tb = probs_t.astype(jnp.bfloat16)
    attended = jnp.einsum(
        "hqk,khd->qhd", probs_b, values, preferred_element_type=jnp.float32
    ).astype(jnp.bfloat16)
    attended_t = jnp.einsum("hqk,khd->qhd", probs_b, values_t, preferred_element_type=jnp.float32)
    attended_t = (
        attended_t
        + jnp.einsum("hqk,khd->qhd", probs_tb, values, preferred_element_type=jnp.float32)
    ).astype(jnp.bfloat16)
    return (attended, attended_t)


def shards(latent, probe, norm_gain, w_query, w_key, w_value, w_out, tile_mask):
    tok_rows, own_cols = latent.shape
    head_cols = w_query.shape[1]
    col_start = lax.axis_index("head") * own_cols
    tangent_own = lax.dynamic_slice_in_dim(probe, col_start, own_cols, 1).astype(jnp.float32)
    latent_f = latent.astype(jnp.float32)
    gain_own = lax.dynamic_slice_in_dim(norm_gain, col_start, own_cols, 0)
    squares, crossed = lax.psum(
        (jnp.sum(latent_f * latent_f, -1), jnp.sum(latent_f * tangent_own, -1)), "head"
    )
    inverse = lax.rsqrt(squares[:, None] / D + 1e-06)
    along = crossed[:, None] / D
    normed_own = (latent_f * inverse * gain_own).astype(jnp.bfloat16)
    normed_t_own = ((tangent_own * inverse - latent_f * inverse**3 * along) * gain_own).astype(
        jnp.bfloat16
    )
    normed, normed_t = (
        lax.all_gather(normed_own, "head", axis=1, tiled=True),
        lax.all_gather(normed_t_own, "head", axis=1, tiled=True),
    )

    def add_rows(weight_rows):
        first = jnp.dot(normed, weight_rows, preferred_element_type=jnp.float32)
        second = jnp.dot(normed_t, weight_rows, preferred_element_type=jnp.float32)
        return (first, second)

    pair_query = add_rows(lax.all_gather(w_query, "ctx", axis=0, tiled=True))
    pair_key = add_rows(lax.all_gather(w_key, "ctx", axis=0, tiled=True))
    pair_value = add_rows(lax.all_gather(w_value, "ctx", axis=0, tiled=True))
    heads_dev = head_cols // HD
    query = pair_query[0].astype(jnp.bfloat16).reshape(tok_rows, heads_dev, HD)
    query_t = pair_query[1].astype(jnp.bfloat16).reshape(tok_rows, heads_dev, HD)
    stacked = jnp.stack(
        [
            pair_key[0].astype(jnp.bfloat16),
            pair_value[0].astype(jnp.bfloat16),
            pair_key[1].astype(jnp.bfloat16),
            pair_value[1].astype(jnp.bfloat16),
        ]
    )
    beside_all = with_halo(stacked, (("ctx", 1),), tok_rows)
    beside_all = beside_all.reshape(4, 3 * tok_rows, heads_dev, HD)
    tiles_dev = tok_rows // TILE
    ctx_slot = lax.axis_index("ctx")
    mask_pad = jnp.pad(tile_mask, tiles_dev)
    tile_rows = lax.dynamic_slice(
        mask_pad,
        (ctx_slot * tiles_dev + tiles_dev, ctx_slot * tiles_dev),
        (tiles_dev, 3 * tiles_dev),
    )
    allowed = jnp.repeat(jnp.repeat(tile_rows, TILE, 0), TILE, 1) == 1
    attended, attended_t = attend_block(
        query, query_t, beside_all[0], beside_all[1], beside_all[2], beside_all[3], allowed
    )
    both_rows = jnp.concatenate(
        [attended.reshape(tok_rows, head_cols), attended_t.reshape(tok_rows, head_cols)], 0
    )
    terms = jnp.dot(
        both_rows,
        lax.all_gather(w_out, "ctx", axis=1, tiled=True),
        preferred_element_type=jnp.float32,
    )
    summed = lax.psum_scatter(
        terms.astype(jnp.bfloat16), "head", scatter_dimension=1, tiled=True
    ).astype(jnp.float32)
    branch = summed[:tok_rows]
    branch_t = summed[tok_rows:]
    mixed = (latent_f + branch).astype(jnp.bfloat16)
    trace_terms = lax.psum(jnp.sum(tangent_own * branch_t, -1), "head")
    return (mixed, branch_t.astype(jnp.bfloat16), trace_terms)


def solution(mesh):
    placed = (
        P("ctx", "head"),
        P("ctx", None),
        P(),
        P("ctx", "head"),
        P("ctx", "head"),
        P("ctx", "head"),
        P("head", "ctx"),
        P(),
    )
    return jax.shard_map(
        shards,
        mesh=mesh,
        in_specs=placed,
        out_specs=(P("ctx", "head"), P("ctx", "head"), P("ctx")),
        check_vma=False,
    )
```

profile of v0, /device:TPU:0, one launch (start us, length us, event | category | flops | bytes accessed | tf_op | source)
XLA Modules:
  0.0 851.1 jit_solution(12549174765315246761)
XLA Ops:
  11.1 5.9 all-reduce.1
  26.1 52.3 %all-gather.7.cloned.1.call-done = bf16[384,5120]{1,0:T(8,128)(2,1)} async-done(((bf16[384,2560]{1,0:T(8,128)(2,1)}), bf16[384,5120]{1,0:T(8,128)(2,1)}) %all-gather.7.cloned.1.call-update) | async-done | bytes 3932176 | tf_op jit(solution)/shard_map/all_gather | solution.py:68
  78.4 122.6 %all-gather.9.cloned.1.call-done = bf16[5120,1536]{1,0:T(8,128)(2,1)} async-done(((bf16[320,1536]{1,0:T(8,128)(2,1)}), bf16[5120,1536]{1,0:T(8,128)(2,1)}) %all-gather.9.cloned.1.call-update) | async-done | bytes 15728656 | tf_op jit(solution)/shard_map/all_gather | solution.py:78
  201.0 10.8 %fusion.18 = bf16[1,384,1536]{2,1,0:T(8,128)(2,1)S(1)} fusion(bf16[384,5120]{1,0:T(8,128)(2,1)} %all-gather.7.cloned.1.call-done, bf16[5120,1536]{1,0:T(8,128)(2,1)} %all-gather.9.cloned.1.call-done), kind=kOutput, calls=%fused_computation.41 | convolution fusion | flops 6040387584 | bytes 20840448 | tf_op jit(solution)/shard_map/dot_general | solution.py:73
  211.8 110.0 %all-gather.11.cloned.1.call-done = bf16[5120,1536]{1,0:T(8,128)(2,1)} async-done(((bf16[320,1536]{1,0:T(8,128)(2,1)}), bf16[5120,1536]{1,0:T(8,128)(2,1)}) %all-gather.11.cloned.1.call-update) | async-done | bytes 15728656 | tf_op jit(solution)/shard_map/all_gather | solution.py:79
  321.8 10.8 %fusion.19 = bf16[1,384,1536]{2,1,0:T(8,128)(2,1)S(1)} fusion(bf16[384,5120]{1,0:T(8,128)(2,1)} %all-gather.7.cloned.1.call-done, bf16[5120,1536]{1,0:T(8,128)(2,1)} %all-gather.11.cloned.1.call-done), kind=kOutput, calls=%fused_computation.42 | convolution fusion | flops 6040387584 | bytes 20840448 | tf_op jit(solution)/shard_map/dot_general | solution.py:73
  332.6 43.2 %all-gather.13.cloned.1.call-done = bf16[384,5120]{1,0:T(8,128)(2,1)} async-done(((bf16[384,2560]{1,0:T(8,128)(2,1)}), bf16[384,5120]{1,0:T(8,128)(2,1)}) %all-gather.13.cloned.1.call-update) | async-done | bytes 3932176 | tf_op jit(solution)/shard_map/all_gather | solution.py:69
  375.8 10.9 %fusion.20 = bf16[1,384,1536]{2,1,0:T(8,128)(2,1)S(1)} fusion(bf16[384,5120]{1,0:T(8,128)(2,1)} %all-gather.13.cloned.1.call-done, bf16[5120,1536]{1,0:T(8,128)(2,1)} %all-gather.9.cloned.1.call-done), kind=kOutput, calls=%fused_computation.43 | convolution fusion | flops 6040387584 | bytes 20840448 | tf_op jit(solution)/shard_map/dot_general | solution.py:74
  389.0 6.2 fusion.21
  407.3 155.1 %all-gather.15.cloned.1.call-done = bf16[5120,1536]{1,0:T(8,128)(2,1)} async-done(((bf16[320,1536]{1,0:T(8,128)(2,1)}), bf16[5120,1536]{1,0:T(8,128)(2,1)}) %all-gather.15.cloned.1.call-update) | async-done | bytes 15728656 | tf_op jit(solution)/shard_map/all_gather | solution.py:77
  562.3 11.6 %convolution_convert_fusion.2 = bf16[384,1536]{1,0:T(8,128)(2,1)} fusion(bf16[384,5120]{1,0:T(8,128)(2,1)} %all-gather.7.cloned.1.call-done, bf16[5120,1536]{1,0:T(8,128)(2,1)} %all-gather.15.cloned.1.call-done), kind=kOutput, calls=%fused_computation.36 | convolution fusion | flops 6040387584 | bytes 20840448 | tf_op jit(solution)/shard_map/dot_general | solution.py:73
  576.3 11.6 %convolution_convert_fusion.1 = bf16[384,1536]{1,0:T(8,128)(2,1)} fusion(bf16[384,5120]{1,0:T(8,128)(2,1)} %all-gather.13.cloned.1.call-done, bf16[5120,1536]{1,0:T(8,128)(2,1)} %all-gather.15.cloned.1.call-done), kind=kOutput, calls=%fused_computation.35 | convolution fusion | flops 6040387584 | bytes 20840448 | tf_op jit(solution)/shard_map/dot_general | solution.py:74
  590.3 5.9 pad_maximum_fusion
  605.7 5.8 copy.20
  611.5 6.1 copy.31
  617.6 5.8 copy.27
  623.4 13.7 %exponential_reduce_fusion = (f32[12,384]{1,0:T(8,128)}, f32[12,384,1152]{2,1,0:T(8,128)}) fusion(bf16[384,12,128]{0,2,1:T(8,128)(2,1)} %bitcast.66, bf16[1152,12,128]{0,2,1:T(8,128)(2,1)S(1)} %bitcast.55, pred[384,1152]{1,0:T(8,128)(4,1)} %copy.22), kind=kOutput, calls=%fused_computation.7 | convolution fusion | flops 1380189312 | bytes 26413056 | tf_op jit(solution)/shard_map/sub | solution.py:31
  637.0 12.8 %fusion.27 = bf16[12,128,384]{2,1,0:T(8,128)(2,1)} fusion(bf16[1152,12,128]{0,2,1:T(8,128)(2,1)} %bitcast.62, f32[12,384]{1,0:T(8,128)} %get-tuple-element.17, bf16[384,12,128]{0,2,1:T(8,128)(2,1)} %bitcast.67, bf16[1152,12,128]{0,2,1:T(8,128)(2,1)S(1)} %bitcast.56, pred[384,1152]{1,0:T(8,128)(4,1)} %copy.22), kind=kOutput, calls=%fused_computation.49 | convolution fusion | flops 2745046528 | bytes 9897984 | tf_op jit(solution)/shard_map/hqk,khd->qhd/dot_general | solution.py:40
  649.9 12.0 %fusion.36 = f32[12,384,1152]{2,1,0:T(8,128)} fusion(bf16[384,12,128]{0,2,1:T(8,128)(2,1)} %bitcast.60, bf16[1152,12,128]{0,2,1:T(8,128)(2,1)S(1)} %bitcast.57), kind=kOutput, calls=%fused_computation.61 | convolution fusion | flops 1358954496 | bytes 25952256 | tf_op jit(solution)/shard_map/qhd,khd->hqk/dot_general | solution.py:33
  661.8 25.8 %multiply_reduce_fusion = (f32[12,384]{1,0:T(8,128)}, f32[12,384,1152]{2,1,0:T(8,128)}) fusion(f32[12,384]{1,0:T(8,128)S(1)} %copy-done.7, f32[12,384,1152]{2,1,0:T(8,128)} %get-tuple-element.18, f32[12,384,1152]{2,1,0:T(8,128)} %fusion.36, bf16[384,12,128]{0,2,1:T(8,128)(2,1)S(1)} %bitcast.70, bf16[1152,12,128]{0,2,1:T(8,128)(2,1)} %bitcast.64), kind=kOutput, calls=%fused_computation.3 | convolution fusion | flops 1385491968 | bytes 68456448 | tf_op jit(solution)/shard_map/qhd,khd->hqk/dot_general | solution.py:35
  687.6 17.3 %fusion.2 = f32[12,128,384]{2,1,0:T(8,128)} fusion(bf16[1152,12,128]{0,2,1:T(8,128)(2,1)} %bitcast.63, f32[12,384,1152]{2,1,0:T(8,128)} %get-tuple-element.20, f32[12,384]{1,0:T(8,128)} %get-tuple-element.19, f32[12,384]{1,0:T(8,128)} %get-tuple-element.17, bf16[384,12,128]{0,2,1:T(8,128)(2,1)} %bitcast.68, bf16[1152,12,128]{0,2,1:T(8,128)(2,1)S(1)} %bitcast.58, ...), kind=kOutput, calls=%fused_computation.9 | convolution fusion | flops 2755073536 | bytes 32329728 | tf_op jit(solution)/shard_map/hqk,khd->qhd/dot_general | solution.py:46
  704.9 13.4 %add_convert_fusion = bf16[12,128,384]{2,1,0:T(8,128)(2,1)} fusion(f32[12,128,384]{2,1,0:T(8,128)} %fusion.2, bf16[1152,12,128]{0,2,1:T(8,128)(2,1)} %bitcast.61, f32[12,384]{1,0:T(8,128)} %get-tuple-element.17, bf16[384,12,128]{0,2,1:T(8,128)(2,1)} %bitcast.69, bf16[1152,12,128]{0,2,1:T(8,128)(2,1)S(1)} %bitcast.59, pred[384,1152]{1,0:T(8,128)(4,1)} %copy.22), kind=kOutput, calls=%fused_computation.48 | convolution fusion | flops 2745636352 | bytes 12257280 | tf_op jit(solution)/shard_map/hqk,khd->qhd/dot_general | solution.py:43
  718.3 18.4 %convolution_convert_fusion = bf16[768,5120]{1,0:T(8,128)(2,1)} fusion(bf16[1536,5120]{0,1:T(8,128)(2,1)} %all-gather.17.cloned.1.call-done, bf16[384,1536]{0,1:T(8,128)(2,1)} %bitcast.74, bf16[384,1536]{0,1:T(8,128)(2,1)} %bitcast.73), kind=kOutput, calls=%fused_computation.11 | convolution fusion | flops 12088246272 | bytes 25952256 | tf_op jit(solution)/shard_map/dot_general | solution.py:108
  736.8 93.2 %reduce-scatter.2.cloned.1.call-done = bf16[768,2560]{1,0:T(8,128)(2,1)} async-done(((bf16[768,5120]{1,0:T(8,128)(2,1)}), bf16[768,2560]{1,0:T(8,128)(2,1)}) %reduce-scatter.2.cloned.1.call-update) | async-done | bytes 3932176 | tf_op jit(solution)/shard_map/reduce_scatter | solution.py:113
  (55 shorter events, 55.4 us)
Async XLA Ops:
  7.2 9.9 %copy-start = (bf16[384,2560]{1,0:T(8,128)(2,1)S(1)}, bf16[384,2560]{1,0:T(8,128)(2,1)}, u32[]{:S(2)}) copy-start(bf16[384,2560]{1,0:T(8,128)(2,1)} %param.8) | copy-start | bytes 5898244
  7.2 71.2 %all-gather.7.cloned.1.call-start = ((), (), s32[]{:S(2)}) async-start(), calls=%async_computation.1 | async-start | bytes 5898240 | tf_op jit(solution)/shard_map/all_gather | solution.py:68
  22.6 178.4 %all-gather.9.cloned.1.call-start = ((), (), s32[]{:S(2)}) async-start(), calls=%async_computation.2 | async-start | bytes 16711680 | tf_op jit(solution)/shard_map/all_gather | solution.py:78
  23.4 298.4 %all-gather.11.cloned.1.call-start = ((), (), s32[]{:S(2)}) async-start(), calls=%async_computation.3 | async-start | bytes 16711680 | tf_op jit(solution)/shard_map/all_gather | solution.py:79
  24.1 351.7 %all-gather.13.cloned.1.call-start = ((), (), s32[]{:S(2)}) async-start(), calls=%async_computation.4 | async-start | bytes 5898240 | tf_op jit(solution)/shard_map/all_gather | solution.py:69
  24.7 537.6 %all-gather.15.cloned.1.call-start = ((), (), s32[]{:S(2)}) async-start(), calls=%async_computation.5 | async-start | bytes 16711680 | tf_op jit(solution)/shard_map/all_gather | solution.py:77
  25.3 693.0 %all-gather.17.cloned.1.call-start = ((), (), s32[]{:S(2)}) async-start(), calls=%async_computation.6 | async-start | bytes 16711680 | tf_op jit(solution)/shard_map/all_gather | solution.py:110
  25.9 804.2 %reduce-scatter.2.cloned.1.call-start = ((), (), s32[]{:S(2)}) async-start(), calls=%async_computation.7 | async-start | bytes 11796480 | tf_op jit(solution)/shard_map/reduce_scatter | solution.py:113
  375.8 11.8 %copy-start.5 = (bf16[5120,1536]{1,0:T(8,128)(2,1)S(1)}, bf16[5120,1536]{1,0:T(8,128)(2,1)}, u32[]{:S(2)}) copy-start(bf16[5120,1536]{1,0:T(8,128)(2,1)} %all-gather.11.cloned.1.call-done) | copy-start | bytes 47185924
  375.8 13.2 %copy-start.6 = (bf16[384,5120]{1,0:T(8,128)(2,1)S(1)}, bf16[384,5120]{1,0:T(8,128)(2,1)}, u32[]{:S(2)}) copy-start(bf16[384,5120]{1,0:T(8,128)(2,1)} %all-gather.13.cloned.1.call-done) | copy-start | bytes 11796484
  395.2 2.6 copy-start.3
  397.8 192.6 %collective-permute-start = (bf16[4,384,1536]{2,1,0:T(8,128)(2,1)}, bf16[4,384,1536]{2,1,0:T(8,128)(2,1)}, u32[]{:S(2)}, u32[]{:S(2)}) collective-permute-start(bf16[4,384,1536]{2,1,0:T(8,128)(2,1)} %pad_maximum_fusion.1), channel_id=1, source_target_pairs={{0,2},{2,4},{4,6},{6,8},{8,10},{10,12},{12,14},{14,16},{16,18},{18... | collective-permute-start | bytes 14155784 | tf_op jit(solution)/shard_map/ppermute | solution.py:16
  401.5 188.8 %collective-permute-start.1 = (bf16[4,384,1536]{2,1,0:T(8,128)(2,1)}, bf16[4,384,1536]{2,1,0:T(8,128)(2,1)}, u32[]{:S(2)}, u32[]{:S(2)}) collective-permute-start(bf16[4,384,1536]{2,1,0:T(8,128)(2,1)} %pad_maximum_fusion.1), channel_id=1, source_target_pairs={{2,0},{4,2},{6,4},{8,6},{10,8},{12,10},{14,12},{16,14},{18,16},{20... | collective-permute-start | bytes 14155784 | tf_op jit(solution)/shard_map/ppermute | solution.py:19
  649.8 12.0 %copy-start.4 = (bf16[384,1536]{0,1:T(8,128)(2,1)S(1)}, bf16[384,1536]{0,1:T(8,128)(2,1)}, u32[]{:S(2)}) copy-start(bf16[384,1536]{0,1:T(8,128)(2,1)} %copy.23) | copy-start | bytes 3538948
  649.9 12.0 %copy-start.7 = (f32[12,384]{1,0:T(8,128)S(1)}, f32[12,384]{1,0:T(8,128)}, u32[]{:S(2)}) copy-start(f32[12,384]{1,0:T(8,128)} %get-tuple-element.17) | copy-start | bytes 55300
  736.8 96.6 %copy-start.1 = (bf16[384,2560]{1,0:T(8,128)(2,1)S(1)}, bf16[384,2560]{1,0:T(8,128)(2,1)}, u32[]{:S(2)}) copy-start(bf16[384,2560]{1,0:T(8,128)(2,1)} %param.8) | copy-start | bytes 5898244
  830.0 3.3 copy-start.2
Sparse Core Ops, SparseCore 0:
  22.8 55.5 all-gather.6
  80.7 120.2 all-gather.8
  203.3 118.4 all-gather.10
  323.8 51.9 all-gather.12
  377.9 184.3 all-gather.14
  564.5 119.2 all-gather.16
  736.9 93.0 reduce-scatter.1
where the time goes:
time: 855 us; the launch traced here: 851 us
  waiting for transfers between devices  579 us (68%)
  matrix products  175 us (20%)
  local copies, waits for them, and re-layouts  41.5 us (5%)
  other arithmetic  23.4 us (3%)
  between operations  14.5 us (2%)
  blocking collectives  11.3 us (1%)
    all_gather x1, waiting for transfers between devices, shards(): pair_query = add_rows(lax.all_gather(w_query, 'ctx', axis=0, tiled=True))  155 us
    all_gather x1, waiting for transfers between devices, shards(): pair_key = add_rows(lax.all_gather(w_key, 'ctx', axis=0, tiled=True))  123 us
    all_gather x1, waiting for transfers between devices, shards(): pair_value = add_rows(lax.all_gather(w_value, 'ctx', axis=0, tiled=True))  110 us
    reduce_scatter x1, waiting for transfers between devices, shards(): lax.psum_scatter(terms.astype(jnp.bfloat16), 'head', scatter_dimension=1,...  93.2 us
    all_gather x1, waiting for transfers between devices, shards(): lax.all_gather(normed_own, 'head', axis=1, tiled=True)  52.3 us
    all_gather x1, waiting for transfers between devices, shards(): lax.all_gather(normed_t_own, 'head', axis=1, tiled=True)  43.2 us
    dot_general x3, matrix products, add_rows(): first = jnp.dot(normed, weight_rows, preferred_element_type=jnp.float32)  33.2 us
    dot_general x3, matrix products, add_rows(): second = jnp.dot(normed_t, weight_rows, preferred_element_type=jnp.float32)  28.8 us
  transfers between devices with their start and end apart: 9, of which 6 were waited for; matrix products, arithmetic and copies ran while one was open for 24% of the time, Pallas kernels for 0%

commit v1 on v0

--- a/solution.py
+++ b/solution.py
@@ -6,6 +6,19 @@
 D = 5120
 HD = 128
 TILE = 128
+
+
+def collect(x, axis, dim):
+    ways = lax.axis_size(axis)
+    up = [(d, (d + 1) % ways) for d in range(ways)]
+    down = [(d, (d - 1) % ways) for d in range(ways)]
+    earlier, later = ([x], [x])
+    for _ in range(ways // 2):
+        earlier.append(lax.ppermute(earlier[-1], axis, up))
+    for _ in range((ways - 1) // 2):
+        later.append(lax.ppermute(later[-1], axis, down))
+    line = jnp.concatenate([*earlier[::-1], *later[1:]], axis=dim)
+    return jnp.roll(line, (lax.axis_index(axis) - ways // 2) * x.shape[dim], axis=dim)
 
 
 def with_halo(block, sides, width):
@@ -76,7 +89,7 @@
 
     pair_query = add_rows(lax.all_gather(w_query, "ctx", axis=0, tiled=True))
     pair_key = add_rows(lax.all_gather(w_key, "ctx", axis=0, tiled=True))
-    pair_value = add_rows(lax.all_gather(w_value, "ctx", axis=0, tiled=True))
+    pair_value = add_rows(collect(w_value, "ctx", 0))
     heads_dev = head_cols // HD
     query = pair_query[0].astype(jnp.bfloat16).reshape(tok_rows, heads_dev, HD)
     query_t = pair_query[1].astype(jnp.bfloat16).reshape(tok_rows, heads_dev, HD)

time: 855 us -> 763 us (0.89)
  waiting for transfers between devices: 579 us -> 317 us
  starting transfers between devices: 5.66 us -> 121 us
  local copies, waits for them, and re-layouts: 41.5 us -> 92.7 us
    all_gather x1, waiting for transfers between devices: 123 us -> 5.97 us  [shards(): pair_key = add_rows(lax.all_gather(w_key, 'ctx', axis=0, tiled=True))]
    ppermute x0 -> x15, starting transfers between devices: none -> 112 us  [the longest x8 103 us: collect(): earlier.append(lax.ppermute(earlier[-1], axis, up))]
    all_gather x1 -> x0, waiting for transfers between devices: 110 us -> none  [shards(): pair_value = add_rows(lax.all_gather(w_value, 'ctx', axis=0, tiled=True))]
    ppermute x0 -> x15, waiting for transfers between devices: none -> 65.9 us  [the longest x8 49.8 us: collect(): earlier.append(lax.ppermute(earlier[-1], axis, up))]
    all_gather x1, waiting for transfers between devices: 52.3 us -> 0.01 us  [shards(): lax.all_gather(normed_own, 'head', axis=1, tiled=True)]
    unnamed x19 -> x82, local copies, waits for them, and re-layouts: 2.36 us -> 52.6 us
    all_gather x1, waiting for transfers between devices: 43.2 us -> 0.02 us  [shards(): lax.all_gather(normed_t_own, 'head', axis=1, tiled=True)]
  transfers between devices with their start and end apart: 9 -> 23, of which waited for: 6 -> 13; matrix products, arithmetic and copies ran while one was open for 24% -> 33% of each run, Pallas kernels for 0% -> 0%
where the time goes in v1:
time: 763 us; the launch traced here: 758 us
  waiting for transfers between devices  317 us (42%)
  matrix products  177 us (23%)
  starting transfers between devices  121 us (16%)
  local copies, waits for them, and re-layouts  92.7 us (12%)
  other arithmetic  23.8 us (3%)
  between operations  14.8 us (2%)
  blocking collectives  11.3 us (1%)
    all_gather x1, waiting for transfers between devices, shards(): pair_query = add_rows(lax.all_gather(w_query, 'ctx', axis=0, tiled=True))  150 us
    ppermute x8, starting transfers between devices, collect(): earlier.append(lax.ppermute(earlier[-1], axis, up))  103 us
    reduce_scatter x1, waiting for transfers between devices, shards(): lax.psum_scatter(terms.astype(jnp.bfloat16), 'head', scatter_dimension=1,...  93.4 us
    unnamed x82, local copies, waits for them, and re-layouts  52.6 us
    ppermute x8, waiting for transfers between devices, collect(): earlier.append(lax.ppermute(earlier[-1], axis, up))  49.8 us
    dot_general x3, matrix products, add_rows(): first = jnp.dot(normed, weight_rows, preferred_element_type=jnp.float32)  34.5 us
    dot_general x3, matrix products, add_rows(): second = jnp.dot(normed_t, weight_rows, preferred_element_type=jnp.float32)  28.8 us
    dot_general x1, matrix products, attend_block(): jnp.einsum('qhd,khd->hqk', queries, keys_t, preferred_element_type=jnp.fl...  25.8 us
  transfers between devices with their start and end apart: 23, of which 13 were waited for; matrix products, arithmetic and copies ran while one was open for 33% of the time, Pallas kernels for 0%

profile of v1, /device:TPU:0, one launch (start us, length us, event | category | flops | bytes accessed | tf_op | source)
XLA Modules:
  0.0 757.8 jit_solution(14548263682084588059)
XLA Ops:
  25.3 16.2 %collective-permute-done = bf16[320,1536]{1,0:T(8,128)(2,1)S(1)} collective-permute-done((bf16[320,1536]{1,0:T(8,128)(2,1)S(1)}, bf16[320,1536]{1,0:T(8,128)(2,1)S(1)}, u32[]{:S(2)}, u32[]{:S(2)}) %collective-permute-start) | collective-permute-done | bytes 983072 | tf_op jit(solution)/shard_map/ppermute | solution.py:17
  46.0 11.9 %collective-permute-done.1 = bf16[320,1536]{1,0:T(8,128)(2,1)S(1)} collective-permute-done((bf16[320,1536]{1,0:T(8,128)(2,1)S(1)}, bf16[320,1536]{1,0:T(8,128)(2,1)S(1)}, u32[]{:S(2)}, u32[]{:S(2)}) %collective-permute-start.1) | collective-permute-done | bytes 983072 | tf_op jit(solution)/shard_map/ppermute | solution.py:17
  62.6 11.6 %collective-permute-done.2 = bf16[320,1536]{1,0:T(8,128)(2,1)S(1)} collective-permute-done((bf16[320,1536]{1,0:T(8,128)(2,1)S(1)}, bf16[320,1536]{1,0:T(8,128)(2,1)S(1)}, u32[]{:S(2)}, u32[]{:S(2)}) %collective-permute-start.2) | collective-permute-done | bytes 983072 | tf_op jit(solution)/shard_map/ppermute | solution.py:17
  74.2 11.7 %collective-permute-start.3 = (bf16[320,1536]{1,0:T(8,128)(2,1)S(1)}, bf16[320,1536]{1,0:T(8,128)(2,1)S(1)}, u32[]{:S(2)}, u32[]{:S(2)}) collective-permute-start(bf16[320,1536]{1,0:T(8,128)(2,1)S(1)} %collective-permute-done.2), channel_id=1, source_target_pairs={{0,2},{2,4},{4,6},{6,8},{8,10},{10,12},{12,14},{14,16},{16,18},{18... | collective-permute-start | bytes 2949128 | tf_op jit(solution)/shard_map/ppermute | solution.py:17
  90.5 18.7 %collective-permute-start.4 = (bf16[320,1536]{1,0:T(8,128)(2,1)S(1)}, bf16[320,1536]{1,0:T(8,128)(2,1)S(1)}, u32[]{:S(2)}, u32[]{:S(2)}) collective-permute-start(bf16[320,1536]{1,0:T(8,128)(2,1)S(1)} %collective-permute-done.3), channel_id=1, source_target_pairs={{0,2},{2,4},{4,6},{6,8},{8,10},{10,12},{12,14},{14,16},{16,18},{18... | collective-permute-start | bytes 2949128 | tf_op jit(solution)/shard_map/ppermute | solution.py:17
  112.3 20.3 %collective-permute-start.5 = (bf16[320,1536]{1,0:T(8,128)(2,1)S(1)}, bf16[320,1536]{1,0:T(8,128)(2,1)S(1)}, u32[]{:S(2)}, u32[]{:S(2)}) collective-permute-start(bf16[320,1536]{1,0:T(8,128)(2,1)S(1)} %collective-permute-done.4), channel_id=1, source_target_pairs={{0,2},{2,4},{4,6},{6,8},{8,10},{10,12},{12,14},{14,16},{16,18},{18... | collective-permute-start | bytes 2949128 | tf_op jit(solution)/shard_map/ppermute | solution.py:17
  134.7 31.3 %collective-permute-start.6 = (bf16[320,1536]{1,0:T(8,128)(2,1)S(1)}, bf16[320,1536]{1,0:T(8,128)(2,1)}, u32[]{:S(2)}, u32[]{:S(2)}) collective-permute-start(bf16[320,1536]{1,0:T(8,128)(2,1)S(1)} %collective-permute-done.5), channel_id=1, source_target_pairs={{0,2},{2,4},{4,6},{6,8},{8,10},{10,12},{12,14},{14,16},{16,18},{18... | collective-permute-start | bytes 2949128 | tf_op jit(solution)/shard_map/ppermute | solution.py:17
  168.3 15.9 %collective-permute-start.7 = (bf16[320,1536]{1,0:T(8,128)(2,1)}, bf16[320,1536]{1,0:T(8,128)(2,1)}, u32[]{:S(2)}, u32[]{:S(2)}) collective-permute-start(bf16[320,1536]{1,0:T(8,128)(2,1)} %collective-permute-done.6), channel_id=1, source_target_pairs={{0,2},{2,4},{4,6},{6,8},{8,10},{10,12},{12,14},{14,16},{16,18},{18... | collective-permute-start | bytes 2949128 | tf_op jit(solution)/shard_map/ppermute | solution.py:17
  184.4 9.4 %collective-permute-done.13 = bf16[320,1536]{1,0:T(8,128)(2,1)} collective-permute-done((bf16[320,1536]{1,0:T(8,128)(2,1)}, bf16[320,1536]{1,0:T(8,128)(2,1)}, u32[]{:S(2)}, u32[]{:S(2)}) %collective-permute-start.13) | collective-permute-done | bytes 983072 | tf_op jit(solution)/shard_map/ppermute | solution.py:19
  253.9 11.6 %fusion.33 = bf16[1,384,1536]{2,1,0:T(8,128)(2,1)S(1)} fusion(bf16[384,5120]{1,0:T(8,128)(2,1)} %all-gather.6.cloned.1.call-done, bf16[10240,1536]{1,0:T(8,128)(2,1)} %constant_dynamic-update-slice_fusion, s32[]{:T(128)S(6)} %select_n.29), kind=kOutput, calls=%fused_computation.48 | convolution fusion | flops 6040387584 | bytes 20840452 | tf_op jit(solution)/shard_map/dot_general | solution.py:86
  265.5 11.0 %fusion.30 = bf16[1,384,1536]{2,1,0:T(8,128)(2,1)S(1)} fusion(bf16[384,5120]{1,0:T(8,128)(2,1)} %all-gather.10.cloned.1.call-done, bf16[10240,1536]{1,0:T(8,128)(2,1)} %constant_dynamic-update-slice_fusion, s32[]{:T(128)S(6)} %select_n.29), kind=kOutput, calls=%fused_computation.47 | convolution fusion | flops 6040387584 | bytes 20840452 | tf_op jit(solution)/shard_map/dot_general | solution.py:87
  282.5 11.3 %fusion.28 = bf16[1,384,1536]{2,1,0:T(8,128)(2,1)S(1)} fusion(bf16[384,5120]{1,0:T(8,128)(2,1)} %all-gather.6.cloned.1.call-done, bf16[5120,1536]{1,0:T(8,128)(2,1)} %all-gather.8.cloned.1.call-done), kind=kOutput, calls=%fused_computation.45 | convolution fusion | flops 6040387584 | bytes 20840448 | tf_op jit(solution)/shard_map/dot_general | solution.py:86
  305.3 8.0 %collective-permute-start.15 = (bf16[4,384,1536]{2,1,0:T(8,128)(2,1)}, bf16[4,384,1536]{2,1,0:T(8,128)(2,1)}, u32[]{:S(2)}, u32[]{:S(2)}) collective-permute-start(bf16[4,384,1536]{2,1,0:T(8,128)(2,1)} %pad_maximum_fusion.1), channel_id=1, source_target_pairs={{0,2},{2,4},{4,6},{6,8},{8,10},{10,12},{12,14},{14,16},{16,18},{18... | collective-permute-start | bytes 14155784 | tf_op jit(solution)/shard_map/ppermute | solution.py:29
  318.9 149.7 %all-gather.12.cloned.1.call-done = bf16[5120,1536]{1,0:T(8,128)(2,1)} async-done(((bf16[320,1536]{1,0:T(8,128)(2,1)}), bf16[5120,1536]{1,0:T(8,128)(2,1)}) %all-gather.12.cloned.1.call-update) | async-done | bytes 15728656 | tf_op jit(solution)/shard_map/all_gather | solution.py:90
  468.6 11.6 %convolution_convert_fusion.2 = bf16[384,1536]{1,0:T(8,128)(2,1)} fusion(bf16[384,5120]{1,0:T(8,128)(2,1)} %all-gather.6.cloned.1.call-done, bf16[5120,1536]{1,0:T(8,128)(2,1)} %all-gather.12.cloned.1.call-done), kind=kOutput, calls=%fused_computation.42 | convolution fusion | flops 6040387584 | bytes 20840448 | tf_op jit(solution)/shard_map/dot_general | solution.py:86
  482.5 11.6 %convolution_convert_fusion.1 = bf16[384,1536]{1,0:T(8,128)(2,1)} fusion(bf16[384,5120]{1,0:T(8,128)(2,1)} %all-gather.10.cloned.1.call-done, bf16[5120,1536]{1,0:T(8,128)(2,1)} %all-gather.12.cloned.1.call-done), kind=kOutput, calls=%fused_computation.41 | convolution fusion | flops 6040387584 | bytes 20840448 | tf_op jit(solution)/shard_map/dot_general | solution.py:87
  529.6 13.6 %exponential_reduce_fusion = (f32[12,384]{1,0:T(8,128)}, f32[12,384,1152]{2,1,0:T(8,128)}) fusion(bf16[384,12,128]{0,2,1:T(8,128)(2,1)} %bitcast.64, bf16[1152,12,128]{0,2,1:T(8,128)(2,1)S(1)} %bitcast.53, pred[384,1152]{1,0:T(8,128)(4,1)} %copy.22), kind=kOutput, calls=%fused_computation.7 | convolution fusion | flops 1380189312 | bytes 26413056 | tf_op jit(solution)/shard_map/sub | solution.py:44
  543.2 12.8 %fusion.41 = bf16[12,128,384]{2,1,0:T(8,128)(2,1)} fusion(bf16[1152,12,128]{0,2,1:T(8,128)(2,1)} %bitcast.60, f32[12,384]{1,0:T(8,128)} %get-tuple-element.17, bf16[384,12,128]{0,2,1:T(8,128)(2,1)} %bitcast.65, bf16[1152,12,128]{0,2,1:T(8,128)(2,1)S(1)} %bitcast.54, pred[384,1152]{1,0:T(8,128)(4,1)} %copy.22), kind=kOutput, calls=%fused_computation.53 | convolution fusion | flops 2745046528 | bytes 9897984 | tf_op jit(solution)/shard_map/hqk,khd->qhd/dot_general | solution.py:53
  556.0 12.0 %fusion.52 = f32[12,384,1152]{2,1,0:T(8,128)} fusion(bf16[384,12,128]{0,2,1:T(8,128)(2,1)} %bitcast.58, bf16[1152,12,128]{0,2,1:T(8,128)(2,1)S(1)} %bitcast.55), kind=kOutput, calls=%fused_computation.99 | convolution fusion | flops 1358954496 | bytes 25952256 | tf_op jit(solution)/shard_map/qhd,khd->hqk/dot_general | solution.py:46
  568.0 25.8 %multiply_reduce_fusion = (f32[12,384]{1,0:T(8,128)}, f32[12,384,1152]{2,1,0:T(8,128)}) fusion(f32[12,384]{1,0:T(8,128)S(1)} %copy-done.23, f32[12,384,1152]{2,1,0:T(8,128)} %get-tuple-element.18, f32[12,384,1152]{2,1,0:T(8,128)} %fusion.52, bf16[384,12,128]{0,2,1:T(8,128)(2,1)S(1)} %bitcast.68, bf16[1152,12,128]{0,2,1:T(8,128)(2,1)} %bitcast.62), kind=kOutput, calls=%fused_computation.3 | convolution fusion | flops 1385491968 | bytes 68456448 | tf_op jit(solution)/shard_map/qhd,khd->hqk/dot_general | solution.py:48
  593.8 17.4 %fusion.6 = f32[12,128,384]{2,1,0:T(8,128)} fusion(bf16[1152,12,128]{0,2,1:T(8,128)(2,1)} %bitcast.61, f32[12,384,1152]{2,1,0:T(8,128)} %get-tuple-element.20, f32[12,384]{1,0:T(8,128)} %get-tuple-element.19, f32[12,384]{1,0:T(8,128)} %get-tuple-element.17, bf16[384,12,128]{0,2,1:T(8,128)(2,1)} %bitcast.66, bf16[1152,12,128]{0,2,1:T(8,128)(2,1)S(1)} %bitcast.56, ...), kind=kOutput, calls=%fused_computation.13 | convolution fusion | flops 2755073536 | bytes 32329728 | tf_op jit(solution)/shard_map/hqk,khd->qhd/dot_general | solution.py:59
  611.3 13.4 %add_convert_fusion = bf16[12,128,384]{2,1,0:T(8,128)(2,1)} fusion(f32[12,128,384]{2,1,0:T(8,128)} %fusion.6, bf16[1152,12,128]{0,2,1:T(8,128)(2,1)} %bitcast.59, f32[12,384]{1,0:T(8,128)} %get-tuple-element.17, bf16[384,12,128]{0,2,1:T(8,128)(2,1)} %bitcast.67, bf16[1152,12,128]{0,2,1:T(8,128)(2,1)S(1)} %bitcast.57, pred[384,1152]{1,0:T(8,128)(4,1)} %copy.22), kind=kOutput, calls=%fused_computation.52 | convolution fusion | flops 2745636352 | bytes 12257280 | tf_op jit(solution)/shard_map/hqk,khd->qhd/dot_general | solution.py:56
  624.7 18.4 %convolution_convert_fusion = bf16[768,5120]{1,0:T(8,128)(2,1)} fusion(bf16[1536,5120]{0,1:T(8,128)(2,1)} %all-gather.14.cloned.1.call-done, bf16[384,1536]{0,1:T(8,128)(2,1)} %bitcast.72, bf16[384,1536]{0,1:T(8,128)(2,1)} %bitcast.71), kind=kOutput, calls=%fused_computation.15 | convolution fusion | flops 12088246272 | bytes 25952256 | tf_op jit(solution)/shard_map/dot_general | solution.py:121
  643.2 93.4 %reduce-scatter.2.cloned.1.call-done = bf16[768,2560]{1,0:T(8,128)(2,1)} async-done(((bf16[768,5120]{1,0:T(8,128)(2,1)}), bf16[768,2560]{1,0:T(8,128)(2,1)}) %reduce-scatter.2.cloned.1.call-update) | async-done | bytes 3932176 | tf_op jit(solution)/shard_map/reduce_scatter | solution.py:126
  (146 shorter events, 174.4 us)
Async XLA Ops:
  7.2 246.8 %all-gather.6.cloned.1.call-start = ((), (), s32[]{:S(2)}) async-start(), calls=%async_computation.1 | async-start | bytes 5898240 | tf_op jit(solution)/shard_map/all_gather | solution.py:81
  23.2 242.4 %all-gather.10.cloned.1.call-start = ((), (), s32[]{:S(2)}) async-start(), calls=%async_computation.3 | async-start | bytes 5898240 | tf_op jit(solution)/shard_map/all_gather | solution.py:82
  23.9 258.6 %all-gather.8.cloned.1.call-start = ((), (), s32[]{:S(2)}) async-start(), calls=%async_computation.2 | async-start | bytes 16711680 | tf_op jit(solution)/shard_map/all_gather | solution.py:91
  24.6 443.9 %all-gather.12.cloned.1.call-start = ((), (), s32[]{:S(2)}) async-start(), calls=%async_computation.4 | async-start | bytes 16711680 | tf_op jit(solution)/shard_map/all_gather | solution.py:90
  25.2 599.5 %all-gather.14.cloned.1.call-start = ((), (), s32[]{:S(2)}) async-start(), calls=%async_computation.5 | async-start | bytes 16711680 | tf_op jit(solution)/shard_map/all_gather | solution.py:123
  25.3 16.3 %collective-permute-start = (bf16[320,1536]{1,0:T(8,128)(2,1)S(1)}, bf16[320,1536]{1,0:T(8,128)(2,1)S(1)}, u32[]{:S(2)}, u32[]{:S(2)}) collective-permute-start(bf16[320,1536]{1,0:T(8,128)(2,1)S(1)} %copy-done.3), channel_id=1, source_target_pairs={{0,2},{2,4},{4,6},{6,8},{8,10},{10,12},{12,14},{14,16},{16,18},{18... | collective-permute-start | bytes 2949128 | tf_op jit(solution)/shard_map/ppermute | solution.py:17
  41.6 16.3 %collective-permute-start.1 = (bf16[320,1536]{1,0:T(8,128)(2,1)S(1)}, bf16[320,1536]{1,0:T(8,128)(2,1)S(1)}, u32[]{:S(2)}, u32[]{:S(2)}) collective-permute-start(bf16[320,1536]{1,0:T(8,128)(2,1)S(1)} %collective-permute-done), channel_id=1, source_target_pairs={{0,2},{2,4},{4,6},{6,8},{8,10},{10,12},{12,14},{14,16},{16,18},{18... | collective-permute-start | bytes 2949128 | tf_op jit(solution)/shard_map/ppermute | solution.py:17
  41.6 21.0 %collective-permute-start.8 = (bf16[320,1536]{1,0:T(8,128)(2,1)S(1)}, bf16[320,1536]{1,0:T(8,128)(2,1)S(1)}, u32[]{:S(2)}, u32[]{:S(2)}) collective-permute-start(bf16[320,1536]{1,0:T(8,128)(2,1)S(1)} %copy-done.3), channel_id=1, source_target_pairs={{0,30},{2,0},{4,2},{6,4},{8,6},{10,8},{12,10},{14,12},{16,14},{18,... | collective-permute-start | bytes 2949128 | tf_op jit(solution)/shard_map/ppermute | solution.py:19
  57.9 16.3 %collective-permute-start.2 = (bf16[320,1536]{1,0:T(8,128)(2,1)S(1)}, bf16[320,1536]{1,0:T(8,128)(2,1)S(1)}, u32[]{:S(2)}, u32[]{:S(2)}) collective-permute-start(bf16[320,1536]{1,0:T(8,128)(2,1)S(1)} %collective-permute-done.1), channel_id=1, source_target_pairs={{0,2},{2,4},{4,6},{6,8},{8,10},{10,12},{12,14},{14,16},{16,18},{18... | collective-permute-start | bytes 2949128 | tf_op jit(solution)/shard_map/ppermute | solution.py:17
  62.6 23.3 %collective-permute-start.9 = (bf16[320,1536]{1,0:T(8,128)(2,1)S(1)}, bf16[320,1536]{1,0:T(8,128)(2,1)S(1)}, u32[]{:S(2)}, u32[]{:S(2)}) collective-permute-start(bf16[320,1536]{1,0:T(8,128)(2,1)S(1)} %collective-permute-done.8), channel_id=1, source_target_pairs={{0,30},{2,0},{4,2},{6,4},{8,6},{10,8},{12,10},{14,12},{16,14},{18,... | collective-permute-start | bytes 2949128 | tf_op jit(solution)/shard_map/ppermute | solution.py:19
  74.2 16.3 %collective-permute-start.3 = (bf16[320,1536]{1,0:T(8,128)(2,1)S(1)}, bf16[320,1536]{1,0:T(8,128)(2,1)S(1)}, u32[]{:S(2)}, u32[]{:S(2)}) collective-permute-start(bf16[320,1536]{1,0:T(8,128)(2,1)S(1)} %collective-permute-done.2), channel_id=1, source_target_pairs={{0,2},{2,4},{4,6},{6,8},{8,10},{10,12},{12,14},{14,16},{16,18},{18... | collective-permute-start | bytes 2949128 | tf_op jit(solution)/shard_map/ppermute | solution.py:17
  85.9 23.3 %collective-permute-start.10 = (bf16[320,1536]{1,0:T(8,128)(2,1)S(1)}, bf16[320,1536]{1,0:T(8,128)(2,1)S(1)}, u32[]{:S(2)}, u32[]{:S(2)}) collective-permute-start(bf16[320,1536]{1,0:T(8,128)(2,1)S(1)} %collective-permute-done.9), channel_id=1, source_target_pairs={{0,30},{2,0},{4,2},{6,4},{8,6},{10,8},{12,10},{14,12},{16,14},{18,... | collective-permute-start | bytes 2949128 | tf_op jit(solution)/shard_map/ppermute | solution.py:19
  90.5 21.7 %collective-permute-start.4 = (bf16[320,1536]{1,0:T(8,128)(2,1)S(1)}, bf16[320,1536]{1,0:T(8,128)(2,1)S(1)}, u32[]{:S(2)}, u32[]{:S(2)}) collective-permute-start(bf16[320,1536]{1,0:T(8,128)(2,1)S(1)} %collective-permute-done.3), channel_id=1, source_target_pairs={{0,2},{2,4},{4,6},{6,8},{8,10},{10,12},{12,14},{14,16},{16,18},{18... | collective-permute-start | bytes 2949128 | tf_op jit(solution)/shard_map/ppermute | solution.py:17
  109.2 23.3 %collective-permute-start.11 = (bf16[320,1536]{1,0:T(8,128)(2,1)S(1)}, bf16[320,1536]{1,0:T(8,128)(2,1)S(1)}, u32[]{:S(2)}, u32[]{:S(2)}) collective-permute-start(bf16[320,1536]{1,0:T(8,128)(2,1)S(1)} %collective-permute-done.10), channel_id=1, source_target_pairs={{0,30},{2,0},{4,2},{6,4},{8,6},{10,8},{12,10},{14,12},{16,14},{18,... | collective-permute-start | bytes 2949128 | tf_op jit(solution)/shard_map/ppermute | solution.py:19
  112.3 22.5 %collective-permute-start.5 = (bf16[320,1536]{1,0:T(8,128)(2,1)S(1)}, bf16[320,1536]{1,0:T(8,128)(2,1)S(1)}, u32[]{:S(2)}, u32[]{:S(2)}) collective-permute-start(bf16[320,1536]{1,0:T(8,128)(2,1)S(1)} %collective-permute-done.4), channel_id=1, source_target_pairs={{0,2},{2,4},{4,6},{6,8},{8,10},{10,12},{12,14},{14,16},{16,18},{18... | collective-permute-start | bytes 2949128 | tf_op jit(solution)/shard_map/ppermute | solution.py:17
  133.5 32.5 %collective-permute-start.12 = (bf16[320,1536]{1,0:T(8,128)(2,1)S(1)}, bf16[320,1536]{1,0:T(8,128)(2,1)}, u32[]{:S(2)}, u32[]{:S(2)}) collective-permute-start(bf16[320,1536]{1,0:T(8,128)(2,1)S(1)} %collective-permute-done.11), channel_id=1, source_target_pairs={{0,30},{2,0},{4,2},{6,4},{8,6},{10,8},{12,10},{14,12},{16,14},{18,... | collective-permute-start | bytes 2949128 | tf_op jit(solution)/shard_map/ppermute | solution.py:19
  134.7 33.6 %collective-permute-start.6 = (bf16[320,1536]{1,0:T(8,128)(2,1)S(1)}, bf16[320,1536]{1,0:T(8,128)(2,1)}, u32[]{:S(2)}, u32[]{:S(2)}) collective-permute-start(bf16[320,1536]{1,0:T(8,128)(2,1)S(1)} %collective-permute-done.5), channel_id=1, source_target_pairs={{0,2},{2,4},{4,6},{6,8},{8,10},{10,12},{12,14},{14,16},{16,18},{18... | collective-permute-start | bytes 2949128 | tf_op jit(solution)/shard_map/ppermute | solution.py:17
  166.0 27.8 %collective-permute-start.13 = (bf16[320,1536]{1,0:T(8,128)(2,1)}, bf16[320,1536]{1,0:T(8,128)(2,1)}, u32[]{:S(2)}, u32[]{:S(2)}) collective-permute-start(bf16[320,1536]{1,0:T(8,128)(2,1)} %collective-permute-done.12), channel_id=1, source_target_pairs={{0,30},{2,0},{4,2},{6,4},{8,6},{10,8},{12,10},{14,12},{16,14},{18,... | collective-permute-start | bytes 2949128 | tf_op jit(solution)/shard_map/ppermute | solution.py:19
  168.3 31.2 %collective-permute-start.7 = (bf16[320,1536]{1,0:T(8,128)(2,1)}, bf16[320,1536]{1,0:T(8,128)(2,1)}, u32[]{:S(2)}, u32[]{:S(2)}) collective-permute-start(bf16[320,1536]{1,0:T(8,128)(2,1)} %collective-permute-done.6), channel_id=1, source_target_pairs={{0,2},{2,4},{4,6},{6,8},{8,10},{10,12},{12,14},{14,16},{16,18},{18... | collective-permute-start | bytes 2949128 | tf_op jit(solution)/shard_map/ppermute | solution.py:17
  184.3 552.3 %reduce-scatter.2.cloned.1.call-start = ((), (), s32[]{:S(2)}) async-start(), calls=%async_computation.6 | async-start | bytes 11796480 | tf_op jit(solution)/shard_map/reduce_scatter | solution.py:126
  193.8 37.8 %collective-permute-start.14 = (bf16[320,1536]{1,0:T(8,128)(2,1)}, bf16[320,1536]{1,0:T(8,128)(2,1)S(1)}, u32[]{:S(2)}, u32[]{:S(2)}) collective-permute-start(bf16[320,1536]{1,0:T(8,128)(2,1)} %collective-permute-done.13), channel_id=1, source_target_pairs={{0,30},{2,0},{4,2},{6,4},{8,6},{10,8},{12,10},{14,12},{16,14},{18,... | collective-permute-start | bytes 2949128 | tf_op jit(solution)/shard_map/ppermute | solution.py:19
  305.3 191.2 %collective-permute-start.15 = (bf16[4,384,1536]{2,1,0:T(8,128)(2,1)}, bf16[4,384,1536]{2,1,0:T(8,128)(2,1)}, u32[]{:S(2)}, u32[]{:S(2)}) collective-permute-start(bf16[4,384,1536]{2,1,0:T(8,128)(2,1)} %pad_maximum_fusion.1), channel_id=1, source_target_pairs={{0,2},{2,4},{4,6},{6,8},{8,10},{10,12},{12,14},{14,16},{16,18},{18... | collective-permute-start | bytes 14155784 | tf_op jit(solution)/shard_map/ppermute | solution.py:29
  313.3 183.2 %collective-permute-start.16 = (bf16[4,384,1536]{2,1,0:T(8,128)(2,1)}, bf16[4,384,1536]{2,1,0:T(8,128)(2,1)}, u32[]{:S(2)}, u32[]{:S(2)}) collective-permute-start(bf16[4,384,1536]{2,1,0:T(8,128)(2,1)} %pad_maximum_fusion.1), channel_id=1, source_target_pairs={{2,0},{4,2},{6,4},{8,6},{10,8},{12,10},{14,12},{16,14},{18,16},{20... | collective-permute-start | bytes 14155784 | tf_op jit(solution)/shard_map/ppermute | solution.py:32
  643.1 96.8 %copy-start = (bf16[384,2560]{1,0:T(8,128)(2,1)S(1)}, bf16[384,2560]{1,0:T(8,128)(2,1)}, u32[]{:S(2)}) copy-start(bf16[384,2560]{1,0:T(8,128)(2,1)} %param.8) | copy-start | bytes 5898244
  (23 other events, 504.6 us)
Sparse Core Ops, SparseCore 0:
  23.3 55.5 all-gather.5
  81.0 53.7 all-gather.9
  137.1 145.2 all-gather.7
  284.6 183.8 all-gather.11
  470.7 119.3 all-gather.13
  643.3 93.2 reduce-scatter.1
